TPU v7x, 32 devices: a whole 2x2x4 slice. The times are simulated.
32 devices in a mesh: wide: 8 (over z, x), narrow: 4 (over y, core).
Axes of the slice: x: 2, y: 2, z: 4, core: 2. Of those that a mesh axis runs over, the one named last changes fastest.
Arguments:
- documents: bfloat16 [2048, 768], P('wide'), may hold values from -6 to 6
- weights: bfloat16 [24576, 768], P(('wide', 'narrow')), may hold values from -6 to 6
- momentum: float32 [24576, 768], P(('wide', 'narrow')), may hold values from -6 to 6
- positives: int32 [2048, 8], P('wide'), may hold values from 0 to 24575
- relocation: int32 [24576], replicated, may hold values from 0 to 24575, each once
- pair_docs: int32 [32, 6], replicated, may hold values from -1 to 15, as said below
- pair_labels: int32 [32, 6], replicated, may hold values from 0 to 2
Outputs:
- new_weights: bfloat16 [24576, 768], P(('wide', 'narrow'))
- new_momentum: float32 [24576, 768], P(('wide', 'narrow'))
- doc_grad: float32 [2048, 768], P('wide', 'narrow')
Inputs may be any that keep to these rules, and one draw needn't show every extreme that they name: `pair_docs`: row i lists pairs of label blocks i * 3 to i * 3 + 2; live entries come first in each row, then -1, and the live (document block, label block) pairs of a row are distinct. Document block b lies on wide index b // 2. The rows of one run of 4 rows starting at a multiple of 4 name exactly 2 distinct wide indices, one document block of each, and at least one of these rows has no -1.
All inputs are finite; a program needn't handle non-finite values.
Results may differ from a plain program's by a relative error of at most 0.0075.
Values may be sent and summed in bfloat16 or wider, within the bound.
A program may use at most 64 MiB of HBM per device.

v0:
```python
import math

import jax
import jax.numpy as jnp
from jax import lax
from jax.sharding import PartitionSpec as P

D = 768
LBLK = 256
DBLK = 128
LB_DEV = 3
POS = 8
DOC_OWN = 2
LAB_DEV = 768


decay_rate = 0.9
step_rate = 0.1


def tile_grad(doc_rows, slot_rows, label_rows, label_ids, row_weight, logit_scale):
    logits = (
        jnp.einsum("nd,ld->nl", doc_rows, label_rows, preferred_element_type=jnp.float32)
        * logit_scale
    )
    target = jnp.any(slot_rows[:, :, None] == label_ids[None, None, :], axis=1).astype(jnp.float32)
    return ((jax.nn.sigmoid(logits) - target) * logit_scale * row_weight).astype(jnp.bfloat16)


def per_device(documents, weights, momentum, positives, relocation, pair_docs, pair_labels):
    wide_count = lax.axis_size("wide")
    narrow_count = lax.axis_size("narrow")
    wide_index = lax.axis_index("wide")
    narrow_index = lax.axis_index("narrow")
    device = wide_index * narrow_count + narrow_index
    pair_count = pair_docs.shape[1]
    fetch_cap = pair_count // LB_DEV
    quarter = D // narrow_count
    logit_scale = 1.0 / math.sqrt(D)
    owners = jnp.arange(wide_count, dtype=jnp.int32)
    group_docs = pair_docs.reshape(wide_count, narrow_count * pair_count)
    group_owner = jnp.where(group_docs >= 0, group_docs // DOC_OWN, -1)
    asked_block = jnp.max(jnp.where(group_owner == wide_index, group_docs % DOC_OWN, -1), axis=1)
    own_owner = lax.dynamic_index_in_dim(group_owner, wide_index, 0, keepdims=False)
    present = jnp.any(own_owner[:, None] == owners[None, :], axis=0)
    position = jnp.cumsum(present.astype(jnp.int32)) - 1
    slot_pick = present[None, :] & (
        position[None, :] == jnp.arange(fetch_cap, dtype=jnp.int32)[:, None]
    )
    owner_list = jnp.sum(jnp.where(slot_pick, owners[None, :], 0), axis=1)
    doc_blocks = documents.reshape(DOC_OWN, DBLK, D)
    slot_blocks = jnp.take(relocation, positives, axis=0).reshape(DOC_OWN, DBLK, POS)
    send_index = jnp.maximum(asked_block, 0)
    send_slots = jnp.take(slot_blocks, send_index, axis=0)
    send_docs = jnp.take(doc_blocks, send_index, axis=0)
    got_docs, got_slots = (
        lax.all_to_all(send_docs, "wide", split_axis=0, concat_axis=0, tiled=True),
        lax.all_to_all(send_slots, "wide", split_axis=0, concat_axis=0, tiled=True),
    )
    fetched = jnp.take(got_docs, owner_list, axis=0)
    fetched_slots = jnp.take(got_slots, owner_list, axis=0)
    docs_row = lax.dynamic_index_in_dim(pair_docs, device, 0, keepdims=False)
    labels_row = lax.dynamic_index_in_dim(pair_labels, device, 0, keepdims=False)
    live_row = docs_row >= 0
    pair_slot = jnp.take(position, jnp.maximum(docs_row // DOC_OWN, 0), axis=0)
    label_base = device * LAB_DEV
    label_range = jnp.arange(LBLK, dtype=jnp.int32)
    doc_rows = fetched.reshape(fetch_cap * DBLK, D)
    slot_rows = fetched_slots.reshape(fetch_cap * DBLK, POS)
    block_range = jnp.arange(fetch_cap, dtype=jnp.int32)
    weight_parts = []
    grad_x = jnp.zeros((fetch_cap * DBLK, D), jnp.float32)
    for label_block in range(LB_DEV):
        chosen = live_row & (labels_row == label_block)
        block_mask = jnp.any(chosen[:, None] & (pair_slot[:, None] == block_range[None, :]), axis=0)
        row_weight = jnp.repeat(block_mask.astype(jnp.float32), DBLK)[:, None]
        label_rows = weights[label_block * LBLK : (label_block + 1) * LBLK]
        label_ids = label_base + label_block * LBLK + label_range
        grad_tile = tile_grad(doc_rows, slot_rows, label_rows, label_ids, row_weight, logit_scale)
        weight_parts.append(
            jnp.einsum("nl,nd->ld", grad_tile, doc_rows, preferred_element_type=jnp.float32)
        )
        grad_x = grad_x + jnp.dot(grad_tile, label_rows, preferred_element_type=jnp.float32)
    grad_w = jnp.concatenate(weight_parts, axis=0)
    grad_x = grad_x.reshape(fetch_cap, DBLK, D)
    partial_value = lax.psum_scatter(
        grad_x.astype(jnp.bfloat16), "narrow", scatter_dimension=2, tiled=True
    ).astype(jnp.float32)
    returning = jnp.where(
        present[:, None, None], jnp.take(partial_value, jnp.maximum(position, 0), axis=0), 0.0
    )
    returned = lax.all_to_all(
        returning.astype(jnp.bfloat16), "wide", split_axis=0, concat_axis=0, tiled=True
    ).astype(returning.dtype)
    picker = (asked_block[None, :] == jnp.arange(DOC_OWN, dtype=jnp.int32)[:, None]).astype(
        jnp.float32
    )
    doc_grad = jnp.einsum("jg,gbd->jbd", picker, returned, precision=lax.Precision.HIGHEST).reshape(
        DOC_OWN * DBLK, quarter
    )
    new_momentum = decay_rate * momentum + grad_w
    new_weights = (weights.astype(jnp.float32) - step_rate * new_momentum).astype(jnp.bfloat16)
    return (new_weights, new_momentum, doc_grad)


def solution(mesh):
    in_specs = (
        P("wide", None),
        P(("wide", "narrow"), None),
        P(("wide", "narrow"), None),
        P("wide", None),
        P(),
        P(),
        P(),
    )
    out_specs = (P(("wide", "narrow"), None), P(("wide", "narrow"), None), P("wide", "narrow"))
    return jax.shard_map(
        per_device, mesh=mesh, in_specs=in_specs, out_specs=out_specs, check_vma=False
    )
```

profile of v0, /device:TPU:0, one launch (start us, length us, event | category | flops | bytes accessed | tf_op | source)
XLA Modules:
  0.0 128.5 jit_solution(9661235141770597443)
XLA Ops:
  7.2 0.8 fusion.36
  8.2 0.7 compare_select_fusion
  9.2 11.8 %gather_fusion.2 = s32[2048]{0:T(1024)S(1)} fusion(s32[24576]{0:T(1024)S(1)} %copy-done.1, s32[2048]{0:T(1024)S(1)} %broadcast_clamp_fusion), kind=kCustom, calls=%fused_computation.2 | custom fusion | bytes 24576 | tf_op jit(solution)/shard_map/jit(_take)/gather | solution.py:52
  21.2 0.6 gather_fusion.3
  21.8 0.7 broadcast_select_fusion.1
  22.5 7.3 %all-to-all-start.1 = ((s32[8,128,8]{1,2,0:T(8,128)}), s32[8,128,8]{1,2,0:T(8,128)S(1)}, u32[]{:S(2)}, u32[]{:S(2)}) async-start(s32[8,128,8]{1,2,0:T(8,128)} %broadcast_select_fusion.1), calls=%async_computation.1 | async-start | bytes 65536 | tf_op jit(solution)/shard_map/all_to_all | solution.py:58
  30.7 0.5 maximum_bitcast_fusion
  31.3 0.6 gather_fusion.5
  32.0 0.6 gather_fusion
  32.6 1.4 %broadcast_select_fusion = bf16[8,128,768]{2,1,0:T(8,128)(2,1)} fusion(bf16[8,128,768]{2,1,0:T(8,128)(2,1)S(1)} %gather_fusion, pred[8]{0:T(512)(128)(4,1)S(1)} %broadcast_compare_fusion.1), kind=kLoop, calls=%fused_computation.12 | loop fusion | flops 786432 | bytes 3145736 | tf_op jit(solution)/shard_map/jit(_take)/select_n | solution.py:55
  34.0 2.4 %all-to-all-done.1 = s32[8,128,8]{1,2,0:T(8,128)S(1)} async-done(((s32[8,128,8]{1,2,0:T(8,128)}), s32[8,128,8]{1,2,0:T(8,128)S(1)}, u32[]{:S(2)}, u32[]{:S(2)}) %all-to-all-start.1) | async-done | bytes 32800 | tf_op jit(solution)/shard_map/all_to_all | solution.py:58
  36.4 3.6 %all-to-all-start = ((bf16[8,128,768]{2,1,0:T(8,128)(2,1)}), bf16[8,128,768]{2,1,0:T(8,128)(2,1)S(1)}, u32[]{:S(2)}, u32[]{:S(2)}) async-start(bf16[8,128,768]{2,1,0:T(8,128)(2,1)} %broadcast_select_fusion), calls=%async_computation | async-start | bytes 3145728 | tf_op jit(solution)/shard_map/all_to_all | solution.py:57
  40.4 0.6 broadcast_bitcast_fusion.3
  41.0 0.6 broadcast_bitcast_fusion.1
  41.7 0.6 broadcast_bitcast_fusion.2
  42.3 0.5 gather_fusion.4
  43.0 2.7 %compare_reduce_fusion.2 = (pred[256,256]{1,0:T(8,128)(4,1)}, pred[256,256]{1,0:T(8,128)(4,1)}, pred[256,256]{1,0:T(8,128)(4,1)}) fusion(s32[256]{0:T(256)S(1)} %iota_add_fusion.2, s32[256,8]{1,0:T(8,128)S(1)} %copy.60, s32[256]{0:T(256)S(1)} %get-tuple-element.20, s32[256]{0:T(256)S(1)} %get-tuple-element.19), kind=kLoop, calls=%fused_computation.11 | loop fusion | flops 2949120 | bytes 207872 | tf_op jit(solution)/shard_map/reduce_or | solution.py:26
  45.7 30.8 %all-to-all-done = bf16[8,128,768]{2,1,0:T(8,128)(2,1)S(1)} async-done(((bf16[8,128,768]{2,1,0:T(8,128)(2,1)}), bf16[8,128,768]{2,1,0:T(8,128)(2,1)S(1)}, u32[]{:S(2)}, u32[]{:S(2)}) %all-to-all-start) | async-done | bytes 1572896 | tf_op jit(solution)/shard_map/all_to_all | solution.py:57
  76.4 0.6 gather_fusion.1
  77.2 1.2 fusion.19
  78.7 0.3 fusion.21
  79.2 0.4 fusion.20
  80.2 0.9 copy.61
  81.5 19.7 %reduce-scatter.2.cloned.1.call-done = bf16[2,128,192]{1,2,0:T(8,128)(2,1)} async-done(((bf16[2,128,768]{1,2,0:T(8,128)(2,1)}), bf16[2,128,192]{1,2,0:T(8,128)(2,1)}) %reduce-scatter.2.cloned.1.call-update) | async-done | bytes 98320 | tf_op jit(solution)/shard_map/reduce_scatter | solution.py:86
  101.2 1.5 %gather_fusion.6 = bf16[8,128,192]{1,2,0:T(8,128)(2,1)S(1)} fusion(bf16[2,128,192]{1,2,0:T(8,128)(2,1)} %reduce-scatter.2.cloned.1.call-done, s32[1024]{0:T(1024)S(1)} %pad_clamp_fusion), kind=kCustom, calls=%fused_computation.6 | custom fusion | bytes 786464 | tf_op jit(solution)/shard_map/jit(_take)/gather | solution.py:90
  102.7 0.9 select_convert_fusion
  103.6 5.5 %all-to-all-start.2 = ((bf16[8,128,192]{1,2,0:T(8,128)(2,1)}), bf16[8,128,192]{1,2,0:T(8,128)(2,1)S(1)}, u32[]{:S(2)}, u32[]{:S(2)}) async-start(bf16[8,128,192]{1,2,0:T(8,128)(2,1)} %select_convert_fusion), calls=%async_computation.3 | async-start | bytes 786432 | tf_op jit(solution)/shard_map/all_to_all | solution.py:92
  109.7 1.1 copy-done.3
  110.8 2.4 %subtract_convert_fusion = (bf16[768,768]{1,0:T(8,128)(2,1)}, f32[768,768]{1,0:T(8,128)}) fusion(bf16[768,768]{1,0:T(8,128)(2,1)S(1)} %copy-done.2, f32[256,768]{1,0:T(8,128)S(1)} %fusion.53, f32[256,768]{1,0:T(8,128)S(1)} %fusion.52, f32[256,768]{1,0:T(8,128)S(1)} %fusion.51, f32[768,768]{1,0:T(8,128)S(1)} %copy-done.3), kind=kLoop, calls=%fused_computation.8 | loop fusion | flops 4718592 | bytes 9437184 | tf_op jit(solution)/shard_map/convert_element_type | solution.py:102
  113.2 7.5 %all-to-all-done.2 = bf16[8,128,192]{1,2,0:T(8,128)(2,1)S(1)} async-done(((bf16[8,128,192]{1,2,0:T(8,128)(2,1)}), bf16[8,128,192]{1,2,0:T(8,128)(2,1)S(1)}, u32[]{:S(2)}, u32[]{:S(2)}) %all-to-all-start.2) | async-done | bytes 393248 | tf_op jit(solution)/shard_map/all_to_all | solution.py:92
  120.6 0.3 fusion.22
  121.0 0.7 copy.67
  (74 shorter events, 4.2 us)
Async XLA Ops:
  7.2 24.8 %copy-start = (bf16[256,768]{1,0:T(8,128)(2,1)S(1)}, bf16[256,768]{1,0:T(8,128)(2,1)}, u32[]{:S(2)}) copy-start(bf16[256,768]{1,0:T(8,128)(2,1)} %param.7) | copy-start | bytes 1179652
  7.2 2.0 %copy-start.1 = (s32[24576]{0:T(1024)S(1)}, s32[24576]{0:T(1024)}, u32[]{:S(2)}) copy-start(s32[24576]{0:T(1024)} %param.11) | copy-start | bytes 294916
  9.2 12.0 %copy-start.7 = (s32[256,8]{0,1:T(8,128)S(1)}, s32[256,8]{0,1:T(8,128)}, u32[]{:S(2)}) copy-start(s32[256,8]{0,1:T(8,128)} %param.10) | copy-start | bytes 24580
  9.2 20.5 %copy-start.6 = (s32[32,6]{0,1:T(8,128)S(1)}, s32[32,6]{0,1:T(8,128)}, u32[]{:S(2)}) copy-start(s32[32,6]{0,1:T(8,128)} %param.12) | copy-start | bytes 2308
  9.2 20.8 %copy-start.8 = (s32[32,6]{0,1:T(8,128)S(1)}, s32[32,6]{0,1:T(8,128)}, u32[]{:S(2)}) copy-start(s32[32,6]{0,1:T(8,128)} %param.13) | copy-start | bytes 2308
  22.5 14.0 %all-to-all-start.1 = ((s32[8,128,8]{1,2,0:T(8,128)}), s32[8,128,8]{1,2,0:T(8,128)S(1)}, u32[]{:S(2)}, u32[]{:S(2)}) async-start(s32[8,128,8]{1,2,0:T(8,128)} %broadcast_select_fusion.1), calls=%async_computation.1 | async-start | bytes 65536 | tf_op jit(solution)/shard_map/all_to_all | solution.py:58
  30.7 0.6 copy-start.12
  36.4 40.0 %all-to-all-start = ((bf16[8,128,768]{2,1,0:T(8,128)(2,1)}), bf16[8,128,768]{2,1,0:T(8,128)(2,1)S(1)}, u32[]{:S(2)}, u32[]{:S(2)}) async-start(bf16[8,128,768]{2,1,0:T(8,128)(2,1)} %broadcast_select_fusion), calls=%async_computation | async-start | bytes 3145728 | tf_op jit(solution)/shard_map/all_to_all | solution.py:57
  40.0 37.1 %copy-start.2 = (bf16[768,768]{1,0:T(8,128)(2,1)S(1)}, bf16[768,768]{1,0:T(8,128)(2,1)}, u32[]{:S(2)}) copy-start(bf16[768,768]{1,0:T(8,128)(2,1)} %param.8) | copy-start | bytes 3538948
  40.0 61.1 %reduce-scatter.2.cloned.1.call-start = ((), (), s32[]{:S(2)}) async-start(), calls=%async_computation.4 | async-start | bytes 491520 | tf_op jit(solution)/shard_map/reduce_scatter | solution.py:86
  77.1 1.5 %copy-start.5 = (pred[256,256]{1,0:T(8,128)(4,1)S(1)}, pred[256,256]{1,0:T(8,128)(4,1)}, u32[]{:S(2)}) copy-start(pred[256,256]{1,0:T(8,128)(4,1)} %get-tuple-element.5) | copy-start | bytes 196612
  77.2 1.5 %copy-start.11 = (f32[256]{0:T(256)S(1)}, f32[256]{0:T(256)}, u32[]{:S(2)}) copy-start(f32[256]{0:T(256)} %broadcast_bitcast_fusion.1) | copy-start | bytes 3076
  78.4 0.8 copy-start.4
  78.4 0.8 copy-start.10
  79.9 1.2 copy-start.9
  79.9 1.3 copy-start.13
  103.6 17.1 %all-to-all-start.2 = ((bf16[8,128,192]{1,2,0:T(8,128)(2,1)}), bf16[8,128,192]{1,2,0:T(8,128)(2,1)S(1)}, u32[]{:S(2)}, u32[]{:S(2)}) async-start(bf16[8,128,192]{1,2,0:T(8,128)(2,1)} %select_convert_fusion), calls=%async_computation.3 | async-start | bytes 786432 | tf_op jit(solution)/shard_map/all_to_all | solution.py:92
  109.1 1.7 %copy-start.3 = (f32[768,768]{1,0:T(8,128)S(1)}, f32[768,768]{1,0:T(8,128)}, u32[]{:S(2)}) copy-start(f32[768,768]{1,0:T(8,128)} %param.9) | copy-start | bytes 7077892
Sparse Core Ops, SparseCore 0:
  81.2 19.8 reduce-scatter.1
where the time goes:
time: 129 us
  waiting for transfers between devices  60.4 us (47%)
  local copies, waits for them, and re-layouts  22.1 us (17%)
  starting transfers between devices  16.4 us (13%)
  between operations  14.5 us (11%)
  other arithmetic  11.2 us (9%)
  matrix products  3.94 us (3%)
    all_to_all x1, waiting for transfers between devices, per_device(): lax.all_to_all(send_docs, 'wide', split_axis=0, concat_axis=0, tiled=True)  30.8 us
    reduce_scatter x1, waiting for transfers between devices, per_device(): lax.psum_scatter(grad_x.astype(jnp.bfloat16), 'narrow', scatter_dimension...  19.7 us
    gather x3, local copies, waits for them, and re-layouts, per_device(): jnp.take(relocation, positives, axis=0).reshape(DOC_OWN, DBLK, POS)  11.9 us
    all_to_all x1, waiting for transfers between devices, per_device(): lax.all_to_all(returning.astype(jnp.bfloat16), 'wide', split_axis=0, conc...  7.46 us
    all_to_all x1, starting transfers between devices, per_device(): lax.all_to_all(send_slots, 'wide', split_axis=0, concat_axis=0, tiled=True)  7.28 us
    all_to_all x1, starting transfers between devices, per_device(): lax.all_to_all(returning.astype(jnp.bfloat16), 'wide', split_axis=0, conc...  5.51 us
    all_to_all x1, starting transfers between devices, per_device(): lax.all_to_all(send_docs, 'wide', split_axis=0, concat_axis=0, tiled=True)  3.58 us
    reduce_or x1, other arithmetic, tile_grad(): jnp.any(slot_rows[:, :, None] == label_ids[None, None, :], axis=1)  2.71 us
  transfers between devices with their start and end apart: 4, of which 4 were waited for; matrix products, arithmetic and copies ran while one was open for 10% of the time, Pallas kernels for 0%

commit v1 on v0

v1 whole, which is shorter than its diff:
```python
import functools
import math

import jax
import jax.numpy as jnp
from jax import lax
from jax.experimental import pallas as pl
from jax.experimental.pallas import tpu as pltpu
from jax.sharding import PartitionSpec as P

LBLK = 256
DBLK = 128

decay_rate = 0.9
step_rate = 0.1

MESH = pl.DeviceIdType.MESH


def remote(src, dst, send_sem, recv_sem, **axis):
    return pltpu.make_async_remote_copy(
        src_ref=src, dst_ref=dst, send_sem=send_sem, recv_sem=recv_sem,
        device_id=axis, device_id_type=MESH)


def kernel(G, N, F, group_ref, row_docs_ref, row_labels_ref, pos_ref, table_ref, docs_ref, w_hbm,
           grad_ref, x_ref, out_ref,
           w_ref, send_buf, recv_buf, slot_buf, slot_recv, xb, slots, asked_buf,
           gq, rs_recv, ret, ret_recv,
           w_sem, s1, r1, s2, r2, s3, r3, s4, r4, s5, r5):
    g = lax.axis_index("wide")
    n = lax.axis_index("narrow")
    D = docs_ref.shape[1]
    own = docs_ref.shape[0] // DBLK
    part = DBLK // N
    feat = D // N
    labels = w_ref.shape[0]
    lb_dev = labels // LBLK
    pos = pos_ref.shape[0]
    scale = 1.0 / math.sqrt(D)

    w_copy = pltpu.make_async_copy(w_hbm, w_ref, w_sem)
    w_copy.start()

    barrier = pltpu.get_barrier_semaphore()
    for k in range(1, G):
        pl.semaphore_signal(barrier, inc=1, device_id={"wide": lax.rem(g + k, G)}, device_id_type=MESH)
    for k in range(1, N):
        pl.semaphore_signal(barrier, inc=1, device_id={"narrow": lax.rem(n + k, N)}, device_id_type=MESH)

    group = group_ref[...]
    asked = jnp.max(jnp.where((group >= 0) & (group // own == g), group % own, -1), axis=1, keepdims=True)
    asked_buf[...] = jnp.broadcast_to(asked, asked_buf.shape)
    quarter = [docs_ref[pl.ds(pl.multiple_of(b * DBLK + n * part, part), part), :] for b in range(own)]
    for d in range(G):
        pick = quarter[0]
        for b in range(1, own):
            pick = jnp.where(asked[d:d + 1, :] == b, quarter[b], pick)
        send_buf[d] = pick

    mine = group_ref[pl.ds(g, 1), :]
    big = jnp.int32(1 << 30)
    blocks = []
    last = jnp.full((1, 1), -1, jnp.int32)
    for j in range(F):
        last = jnp.min(jnp.where(mine > last, mine, big), axis=1, keepdims=True)
        blocks.append(last)

    pl.semaphore_wait(barrier, G - 1 + N - 1)

    wide_copies = []
    for k in range(1, G):
        to = lax.rem(g + k, G)
        copy = remote(send_buf.at[to], recv_buf.at[g], s1.at[k], r1.at[k], wide=to)
        copy.start()
        wide_copies.append(copy)

    table = table_ref[...]
    height = table.shape[0]
    pieces = []
    top = height * 128 - 1
    shift = 0
    while (top >> shift) > 0:
        pieces.append(((table >> shift) & 255).astype(jnp.float32).astype(jnp.bfloat16))
        shift += 8
    n_docs = docs_ref.shape[0]
    hi_iota = lax.broadcasted_iota(jnp.int32, (height, n_docs), 0)
    lo_iota = lax.broadcasted_iota(jnp.int32, (128, n_docs), 0)
    for p in range(pos):
        ids = pos_ref[p:p + 1, :]
        hot = jnp.where(hi_iota == ids // 128, 1.0, 0.0).astype(jnp.bfloat16)
        low = lo_iota == ids % 128
        total = jnp.zeros((1, n_docs), jnp.float32)
        for i, piece in enumerate(pieces):
            rows = lax.dot_general(piece, hot, (((0,), (0,)), ((), ())), preferred_element_type=jnp.float32)
            total = total + jnp.sum(jnp.where(low, rows, 0.0), axis=0, keepdims=True) * float(1 << (8 * i))
        slot_buf[p:p + 1, :] = total.astype(jnp.int32)

    slot_recv[g] = slot_buf[...]
    recv_buf[g] = send_buf[g]
    for k in range(1, G):
        to = lax.rem(g + k, G)
        copy = remote(slot_buf, slot_recv.at[g], s2.at[k], r2.at[k], wide=to)
        copy.start()
        wide_copies.append(copy)
    for copy in wide_copies:
        copy.wait_recv()

    for j in range(F):
        owner = blocks[j] // own
        local = blocks[j] % own
        pick = recv_buf[0]
        spick = slot_recv[0]
        for s in range(1, G):
            pick = jnp.where(owner == s, recv_buf[s], pick)
            spick = jnp.where(owner == s, slot_recv[s], spick)
        xb[j, n] = pick
        chosen = spick[:, :DBLK]
        for b in range(1, own):
            chosen = jnp.where(local == b, spick[:, b * DBLK:(b + 1) * DBLK], chosen)
        slots[:, j * DBLK:(j + 1) * DBLK] = chosen

    narrow_copies = []
    for k in range(1, N):
        to = lax.rem(n + k, N)
        copy = remote(xb.at[:, n], xb.at[:, n], s3.at[k], r3.at[k], narrow=to)
        copy.start()
        narrow_copies.append(copy)

    w_copy.wait()
    for copy in narrow_copies:
        copy.wait_recv()

    row_docs = row_docs_ref[pl.ds(g * N + n, 1), :]
    row_labels = row_labels_ref[pl.ds(g * N + n, 1), :]
    label_base = (g * N + n) * labels
    step = 2 if F % 2 == 0 else 1
    width = step * DBLK
    lane_block = lax.broadcasted_iota(jnp.int32, (1, width), 1) // DBLK
    for j0 in range(0, F, step):
        x = xb[j0:j0 + step].reshape(width, D)
        x_ref[j0 * DBLK:j0 * DBLK + width, :] = x
        chosen_slots = slots[:, j0 * DBLK:j0 * DBLK + width]
        for c in range(lb_dev):
            weight = jnp.zeros((1, width), jnp.float32)
            for jj in range(step):
                live = jnp.max(
                    jnp.where((row_docs == blocks[j0 + jj]) & (row_labels == c), 1.0, 0.0),
                    axis=1, keepdims=True)
                weight = jnp.where(lane_block == jj, live, weight)
            logits = lax.dot_general(
                w_ref[c * LBLK:(c + 1) * LBLK, :], x, (((1,), (1,)), ((), ())),
                preferred_element_type=jnp.float32) * scale
            ids = lax.broadcasted_iota(jnp.int32, (LBLK, width), 0) + (label_base + c * LBLK)
            hit = ids == chosen_slots[0:1, :]
            for p in range(1, pos):
                hit = hit | (ids == chosen_slots[p:p + 1, :])
            target = jnp.where(hit, 1.0, 0.0)
            grad = ((jax.nn.sigmoid(logits) - target) * scale * weight).astype(jnp.bfloat16)
            grad_ref[c * LBLK:(c + 1) * LBLK, j0 * DBLK:j0 * DBLK + width] = grad
        tile = grad_ref[:, j0 * DBLK:j0 * DBLK + width]
        gx = lax.dot_general(w_ref[...], tile, (((0,), (0,)), ((), ())), preferred_element_type=jnp.float32)
        gq[:, :, j0 * DBLK:j0 * DBLK + width] = gx.astype(jnp.bfloat16).reshape(N, feat, width)

    rs_copies = []
    for k in range(1, N):
        to = lax.rem(n + k, N)
        copy = remote(gq.at[to], rs_recv.at[n], s4.at[k], r4.at[k], narrow=to)
        copy.start()
        rs_copies.append(copy)
    for copy in rs_copies:
        copy.wait_recv()
    total = gq[n].astype(jnp.float32)
    for k in range(1, N):
        total = total + rs_recv[lax.rem(n + k, N)].astype(jnp.float32)
    for d in range(G):
        back = jnp.zeros((feat, DBLK), jnp.float32)
        for j in range(F):
            back = jnp.where(blocks[j] // own == d, total[:, j * DBLK:(j + 1) * DBLK], back)
        ret[d] = back.astype(jnp.bfloat16)

    ret_copies = []
    for k in range(1, G):
        to = lax.rem(g + k, G)
        copy = remote(ret.at[to], ret_recv.at[g], s5.at[k], r5.at[k], wide=to)
        copy.start()
        ret_copies.append(copy)
    ret_recv[g] = ret[g]
    for copy in ret_copies:
        copy.wait_recv()
    sums = [jnp.zeros((feat, DBLK), jnp.float32) for _ in range(own)]
    for s in range(G):
        value = ret_recv[s].astype(jnp.float32)
        who = asked_buf[s:s + 1, :]
        for b in range(own):
            sums[b] = sums[b] + jnp.where(who == b, value, 0.0)
    for b in range(own):
        out_ref[:, b * DBLK:(b + 1) * DBLK] = sums[b]

    for copy in wide_copies + narrow_copies + rs_copies + ret_copies:
        copy.wait_send()


def per_device(documents, weights, momentum, positives, relocation, pair_docs, pair_labels):
    G = lax.axis_size("wide")
    N = lax.axis_size("narrow")
    labels, D = weights.shape
    lb_dev = labels // LBLK
    F = pair_docs.shape[1] // lb_dev
    docs = documents.shape[0]
    feat = D // N
    part = DBLK // N
    pos = positives.shape[1]
    group = pair_docs.reshape(G, -1)
    table = relocation.reshape(-1, 128)
    vmem = pl.BlockSpec(memory_space=pltpu.VMEM)
    dma = pltpu.SemaphoreType.DMA
    bf16 = jnp.bfloat16
    grad, x, out = pl.pallas_call(
        functools.partial(kernel, G, N, F),
        out_shape=(
            jax.ShapeDtypeStruct((labels, F * DBLK), bf16),
            jax.ShapeDtypeStruct((F * DBLK, D), bf16),
            jax.ShapeDtypeStruct((feat, docs), jnp.float32),
        ),
        in_specs=[vmem] * 6 + [pl.BlockSpec(memory_space=pl.ANY)],
        out_specs=(vmem, vmem, vmem),
        scratch_shapes=[
            pltpu.VMEM((labels, D), bf16),
            pltpu.VMEM((G, part, D), bf16),
            pltpu.VMEM((G, part, D), bf16),
            pltpu.VMEM((pos, docs), jnp.int32),
            pltpu.VMEM((G, pos, docs), jnp.int32),
            pltpu.VMEM((F, N, part, D), bf16),
            pltpu.VMEM((pos, F * DBLK), jnp.int32),
            pltpu.VMEM((G, 128), jnp.int32),
            pltpu.VMEM((N, feat, F * DBLK), bf16),
            pltpu.VMEM((N, feat, F * DBLK), bf16),
            pltpu.VMEM((G, feat, DBLK), bf16),
            pltpu.VMEM((G, feat, DBLK), bf16),
            dma,
            dma((G,)), dma((G,)), dma((G,)), dma((G,)),
            dma((N,)), dma((N,)), dma((N,)), dma((N,)),
            dma((G,)), dma((G,)),
        ],
        compiler_params=pltpu.CompilerParams(
            collective_id=0, has_side_effects=True, vmem_limit_bytes=48 << 20),
    )(group, pair_docs, pair_labels, positives.T, table, documents, weights)
    grad_w = jnp.dot(grad, x, preferred_element_type=jnp.float32)
    new_momentum = decay_rate * momentum + grad_w
    new_weights = (weights.astype(jnp.float32) - step_rate * new_momentum).astype(jnp.bfloat16)
    return (new_weights, new_momentum, out.T)


def solution(mesh):
    in_specs = (
        P("wide", None),
        P(("wide", "narrow"), None),
        P(("wide", "narrow"), None),
        P("wide", None),
        P(),
        P(),
        P(),
    )
    out_specs = (P(("wide", "narrow"), None), P(("wide", "narrow"), None), P("wide", "narrow"))
    return jax.shard_map(
        per_device, mesh=mesh, in_specs=in_specs, out_specs=out_specs, check_vma=False
    )
```

time: 129 us -> 48.5 us (0.38)
  the two profiles are of different devices: /device:TPU:0 before, /device:TPU:29 now
where the time goes in v1:
time: 48.5 us; the launch traced here: 48.2 us
  Pallas kernels  37.2 us (77%)
  local copies, waits for them, and re-layouts  6.14 us (13%)
  matrix products  4.16 us (9%)
  between operations  0.64 us (1%)
    pallas_call x1, Pallas kernels, per_device(): pl.pallas_call(functools.partial(kernel, G, N, F), out_shape=(jax.ShapeDt...  37.2 us
    unnamed x11, local copies, waits for them, and re-layouts  6.07 us
    dot_general x1, matrix products, per_device(): grad_w = jnp.dot(grad, x, preferred_element_type=jnp.float32)  4.16 us

profile of v1, /device:TPU:29, one launch (start us, length us, event | category | flops | bytes accessed | tf_op | source)
XLA Modules:
  0.0 48.2 jit_solution(12137277701322603972)
XLA Ops:
  0.6 0.8 %copy.13.row_docs_ref = s32[32,6]{1,0:T(8,128)S(1)} copy(s32[32,6]{0,1:T(8,128)} %param.12) | data formatting | bytes 1536 | tf_op args[5]
  1.4 0.1 reshape.12.group_ref
  1.5 0.8 %copy.15.row_labels_ref = s32[32,6]{1,0:T(8,128)S(1)} copy(s32[32,6]{0,1:T(8,128)} %param.13) | data formatting | bytes 1536 | tf_op args[6]
  2.2 0.0 copy-start
  2.2 1.3 %copy-done = bf16[768,768]{1,0:T(8,128)(2,1)S(1)} copy-done((bf16[768,768]{1,0:T(8,128)(2,1)S(1)}, bf16[768,768]{1,0:T(8,128)(2,1)}, u32[]{:S(2)}) %copy-start) | copy-done | bytes 1179672
  3.5 0.0 copy-start.1
  3.5 1.0 %copy-done.1 = bf16[256,768]{1,0:T(8,128)(2,1)S(1)} copy-done((bf16[256,768]{1,0:T(8,128)(2,1)S(1)}, bf16[256,768]{1,0:T(8,128)(2,1)}, u32[]{:S(2)}) %copy-start.1) | copy-done | bytes 393240
  4.5 0.0 copy-start.2
  4.5 0.9 %copy-done.2 = s32[24576]{0:T(1024)S(1)} copy-done((s32[24576]{0:T(1024)S(1)}, s32[24576]{0:T(1024)}, u32[]{:S(2)}) %copy-start.2) | copy-done | bytes 98328
  5.4 0.0 copy-start.3
  5.4 0.7 %copy-done.3 = s32[256,8]{0,1:T(8,128)S(1)} copy-done((s32[256,8]{0,1:T(8,128)S(1)}, s32[256,8]{0,1:T(8,128)}, u32[]{:S(2)}) %copy-start.3) | copy-done | bytes 8216
  6.1 37.2 %shard_map.94 = (bf16[768,256]{1,0:T(8,128)(2,1)S(1)}, bf16[256,768]{1,0:T(8,128)(2,1)S(1)}, f32[192,256]{1,0:T(8,128)S(1)}) custom-call(s32[8,24]{1,0:T(8,128)S(1)} %reshape.12.group_ref, s32[32,6]{1,0:T(8,128)S(1)} %copy.13.row_docs_ref, s32[32,6]{1,0:T(8,128)S(1)} %copy.15.row_labels_ref, s32[8,256]{1,0:T(8,128)S(1)} %bitcast.7, s32[192,128]{1,0:T(8,128)S(1)} %bitcast.6, ...), custom_call_target="tpu_custom_call" | custom-call | tf_op jit(solution)/shard_map/pallas_call | solution.py:219
  43.3 4.2 %subtract_convert_fusion = (bf16[768,768]{1,0:T(8,128)(2,1)}, f32[768,768]{1,0:T(8,128)}) fusion(bf16[768,768]{1,0:T(8,128)(2,1)S(1)} %copy-done, bf16[768,256]{1,0:T(8,128)(2,1)S(1)} %get-tuple-element.6, bf16[256,768]{1,0:T(8,128)(2,1)S(1)} %get-tuple-element.7, f32[768,768]{1,0:T(8,128)} %param.9), kind=kOutput, calls=%fused_computation | convolution fusion | flops 305528832 | bytes 7864320 | tf_op jit(solution)/shard_map/dot_general | solution.py:249
  47.5 0.7 %copy.17 = f32[256,192]{0,1:T(8,128)} copy(f32[256,192]{0,1:T(8,128)S(1)} %bitcast.5) | data formatting | bytes 393216
Async XLA Ops:
  2.2 1.3 %copy-start = (bf16[768,768]{1,0:T(8,128)(2,1)S(1)}, bf16[768,768]{1,0:T(8,128)(2,1)}, u32[]{:S(2)}) copy-start(bf16[768,768]{1,0:T(8,128)(2,1)} %w_hbm.1) | copy-start | bytes 3538948
  3.5 1.0 %copy-start.1 = (bf16[256,768]{1,0:T(8,128)(2,1)S(1)}, bf16[256,768]{1,0:T(8,128)(2,1)}, u32[]{:S(2)}) copy-start(bf16[256,768]{1,0:T(8,128)(2,1)} %docs_ref.1) | copy-start | bytes 1179652
  4.5 0.9 %copy-start.2 = (s32[24576]{0:T(1024)S(1)}, s32[24576]{0:T(1024)}, u32[]{:S(2)}) copy-start(s32[24576]{0:T(1024)} %param.11) | copy-start | bytes 294916
  5.4 0.7 %copy-start.3 = (s32[256,8]{0,1:T(8,128)S(1)}, s32[256,8]{0,1:T(8,128)}, u32[]{:S(2)}) copy-start(s32[256,8]{0,1:T(8,128)} %param.10) | copy-start | bytes 24580

commit v2 on v1

v2 whole, which is shorter than its diff:
```python
import functools
import math

import jax
import jax.numpy as jnp
from jax import lax
from jax.experimental import pallas as pl
from jax.experimental.pallas import tpu as pltpu
from jax.sharding import PartitionSpec as P

LBLK = 256
DBLK = 128
CHUNKS = 2

decay_rate = 0.9
step_rate = 0.1

MESH = pl.DeviceIdType.MESH


def remote(src, dst, send_sem, recv_sem, **axis):
    return pltpu.make_async_remote_copy(
        src_ref=src, dst_ref=dst, send_sem=send_sem, recv_sem=recv_sem,
        device_id=axis, device_id_type=MESH)


def kernel(G, N, F, docs_hbm, pos_hbm, table_hbm, pd_hbm, pl_hbm, w_hbm, m_hbm,
           new_w_ref, new_m_ref, out_ref,
           docs_ref, pos_ref, table_ref, pd_ref, pl_ref, w_ref,
           send_buf, recv_buf, slot_buf, slot_recv, xb, slots, asked_buf, grad_ref,
           gq, rs1, mid, rs2, ret, ret_recv,
           in_sem, ws, wr, ss, sr, as_, ar, bs, br, cs, cr, ds_, dr, es, er, fs, fr):
    g = lax.axis_index("wide")
    n = lax.axis_index("narrow")
    D = docs_ref.shape[1]
    own = docs_ref.shape[0] // DBLK
    half = DBLK // CHUNKS
    part = half // N
    feat = D // N
    labels = w_ref.shape[0]
    lb_dev = labels // LBLK
    pos = pos_ref.shape[0]
    scale = 1.0 / math.sqrt(D)
    outer = N // 2
    partner = n + 1 - 2 * (n % 2)
    sent = []

    barrier = pltpu.get_barrier_semaphore()
    for k in range(1, G):
        pl.semaphore_signal(barrier, inc=1, device_id={"wide": lax.rem(g + k, G)}, device_id_type=MESH)
    for k in range(1, N):
        pl.semaphore_signal(barrier, inc=1, device_id={"narrow": lax.rem(n + k, N)}, device_id_type=MESH)

    loads = [
        pltpu.make_async_copy(src, dst, in_sem.at[i])
        for i, (src, dst) in enumerate((
            (pd_hbm, pd_ref), (pl_hbm, pl_ref), (docs_hbm, docs_ref), (pos_hbm, pos_ref),
            (table_hbm, table_ref), (w_hbm, w_ref), (m_hbm, new_m_ref)))
    ]
    for load in loads:
        load.start()
    loads[0].wait()
    loads[1].wait()

    pair_docs = pd_ref[...]
    pair_labels = pl_ref[...]
    device_of = lax.broadcasted_iota(jnp.int32, pair_docs.shape, 1)
    group_of = device_of // N
    local = jnp.where((pair_docs >= 0) & (pair_docs // own == g), pair_docs % own, -1)

    def least(x):
        return jnp.min(jnp.min(x, axis=0, keepdims=True), axis=1, keepdims=True)

    def largest(x):
        return jnp.max(jnp.max(x, axis=0, keepdims=True), axis=1, keepdims=True)

    asked = [largest(jnp.where(group_of == d, local, -1)) for d in range(G)]
    big = jnp.int32(1 << 30)
    mine = jnp.where(group_of == g, pair_docs, -1)
    blocks = []
    last = jnp.full((1, 1), -1, jnp.int32)
    for j in range(F):
        last = least(jnp.where(mine > last, mine, big))
        blocks.append(last)
    owner = [b // own for b in blocks]

    loads[2].wait()
    for h in range(CHUNKS):
        rows = [
            docs_ref[pl.ds(pl.multiple_of(b * DBLK + h * half + n * part, part), part), :]
            for b in range(own)]
        for d in range(G):
            pick = rows[0]
            for b in range(1, own):
                pick = jnp.where(asked[d] == b, rows[b], pick)
            send_buf[h, d] = pick
    for d in range(G):
        asked_buf[d:d + 1, :] = jnp.broadcast_to(asked[d], (1, asked_buf.shape[1]))

    loads[3].wait()
    loads[4].wait()
    table = table_ref[...]
    height = table.shape[0]
    pieces = []
    shift = 0
    while ((height * 128 - 1) >> shift) > 0:
        pieces.append(((table >> shift) & 255).astype(jnp.float32).astype(jnp.bfloat16))
        shift += 8
    n_docs = docs_ref.shape[0]
    hi_iota = lax.broadcasted_iota(jnp.int32, (height, n_docs), 0)
    lo_iota = lax.broadcasted_iota(jnp.int32, (128, n_docs), 0)
    for p in range(pos):
        ids = pos_ref[p:p + 1, :]
        hot = jnp.where(hi_iota == ids // 128, 1.0, 0.0).astype(jnp.bfloat16)
        low = lo_iota == ids % 128
        total = jnp.zeros((1, n_docs), jnp.float32)
        for i, piece in enumerate(pieces):
            rows = lax.dot_general(piece, hot, (((0,), (0,)), ((), ())), preferred_element_type=jnp.float32)
            total = total + jnp.sum(jnp.where(low, rows, 0.0), axis=0, keepdims=True) * float(1 << (8 * i))
        slot_buf[p:p + 1, :] = total.astype(jnp.int32)

    pl.semaphore_wait(barrier, G - 1 + N - 1)

    slot_copies = []
    for k in range(1, G):
        to = lax.rem(g + k, G)
        copy = remote(slot_buf, slot_recv.at[g], ss.at[k], sr.at[k], wide=to)
        copy.start()
        slot_copies.append(copy)
    wide_copies = []
    for h in range(CHUNKS):
        copies = []
        for k in range(1, G):
            to = lax.rem(g + k, G)
            copy = remote(send_buf.at[h, to], recv_buf.at[h, g], ws.at[h, k], wr.at[h, k], wide=to)
            copy.start()
            copies.append(copy)
        wide_copies.append(copies)
        sent.extend(copies)
    sent.extend(slot_copies)
    slot_recv[g] = slot_buf[...]
    for h in range(CHUNKS):
        recv_buf[h, g] = send_buf[h, g]

    def take_wide(h):
        for copy in wide_copies[h]:
            copy.wait_recv()
        for j in range(F):
            pick = recv_buf[h, 0]
            for s in range(1, G):
                pick = jnp.where(owner[j] == s, recv_buf[h, s], pick)
            xb[h, j, n] = pick

    def take_slots():
        for copy in slot_copies:
            copy.wait_recv()
        for j in range(F):
            spick = slot_recv[0]
            for s in range(1, G):
                spick = jnp.where(owner[j] == s, slot_recv[s], spick)
            chosen = spick[:, :DBLK]
            for b in range(1, own):
                chosen = jnp.where(blocks[j] % own == b, spick[:, b * DBLK:(b + 1) * DBLK], chosen)
            for h in range(CHUNKS):
                slots[h, :, j * half:(j + 1) * half] = chosen[:, h * half:(h + 1) * half]

    def gather_send(h):
        piece = xb.at[h, :, n]
        across = []
        for k in range(1, outer):
            copy = remote(piece, piece, bs.at[h, k], br.at[h, k], narrow=lax.rem(n + 2 * k, N))
            copy.start()
            across.append(copy)
        near = remote(piece, piece, as_.at[h], ar.at[h], narrow=partner)
        near.start()
        sent.extend(across + [near])
        return across, near

    def gather_forward(h, across):
        passed = []
        for k in range(1, outer):
            across[k - 1].wait_recv()
            piece = xb.at[h, :, lax.rem(n + N - 2 * k, N)]
            copy = remote(piece, piece, cs.at[h, k], cr.at[h, k], narrow=partner)
            copy.start()
            passed.append(copy)
        sent.extend(passed)
        return passed

    me = g * N + n
    label_base = me * labels
    step = 4 if F % 4 == 0 else 2 if F % 2 == 0 else 1
    width = step * half
    span = F * half
    lane_block = lax.broadcasted_iota(jnp.int32, (1, width), 1) // half
    live = [[
        largest(jnp.where((pair_docs == blocks[j]) & (pair_labels == c) & (device_of == me), 1.0, 0.0))
        for c in range(lb_dev)] for j in range(F)]

    def compute(h):
        for j0 in range(0, F, step):
            x = xb[h, j0:j0 + step].reshape(width, D)
            at = h * span + j0 * half
            chosen_slots = slots[h, :, j0 * half:j0 * half + width]
            for c in range(lb_dev):
                weight = live[j0][c]
                for jj in range(1, step):
                    weight = jnp.where(lane_block == jj, live[j0 + jj][c], weight)
                logits = lax.dot_general(
                    w_ref[c * LBLK:(c + 1) * LBLK, :], x, (((1,), (1,)), ((), ())),
                    preferred_element_type=jnp.float32) * scale
                ids = lax.broadcasted_iota(jnp.int32, (LBLK, width), 0) + (label_base + c * LBLK)
                hit = ids == chosen_slots[0:1, :]
                for p in range(1, pos):
                    hit = hit | (ids == chosen_slots[p:p + 1, :])
                target = jnp.where(hit, 1.0, 0.0)
                grad = ((jax.nn.sigmoid(logits) - target) * scale * weight).astype(jnp.bfloat16)
                grad_ref[c * LBLK:(c + 1) * LBLK, at:at + width] = grad
            gx = lax.dot_general(
                w_ref[...], grad_ref[:, at:at + width], (((0,), (0,)), ((), ())),
                preferred_element_type=jnp.float32)
            gq[h, :, :, j0 * half:j0 * half + width] = gx.astype(jnp.bfloat16).reshape(N, feat, width)

    def reduce_first(h):
        copies = []
        for k in reversed(range(outer)):
            copy = remote(gq.at[h, lax.rem(partner + 2 * k, N)], rs1.at[h, k], ds_.at[h, k], dr.at[h, k],
                          narrow=partner)
            copy.start()
            copies.append(copy)
        sent.extend(copies)
        return copies[::-1]

    def reduce_second(h, first):
        copies = []
        for k in range(1, outer):
            first[k].wait_recv()
            to = lax.rem(n + 2 * k, N)
            mid[h, k] = (gq[h, to].astype(jnp.float32) + rs1[h, k].astype(jnp.float32)).astype(jnp.bfloat16)
            copy = remote(mid.at[h, k], rs2.at[h, k], es.at[h, k], er.at[h, k], narrow=to)
            copy.start()
            copies.append(copy)
        sent.extend(copies)
        return copies

    def send_back(h, first, second):
        first[0].wait_recv()
        total = gq[h, n].astype(jnp.float32) + rs1[h, 0].astype(jnp.float32)
        for k in range(1, outer):
            second[k - 1].wait_recv()
            total = total + rs2[h, k].astype(jnp.float32)
        total = total.astype(jnp.bfloat16)
        rows = feat // CHUNKS
        packed = [
            jnp.concatenate(
                [total[i * rows:(i + 1) * rows, j * half:(j + 1) * half] for i in range(CHUNKS)], axis=1)
            for j in range(F)]
        for d in range(G):
            back = jnp.zeros((rows, DBLK), jnp.bfloat16)
            for j in range(F):
                back = jnp.where(owner[j] == d, packed[j], back)
            ret[h, d] = back
        copies = []
        for k in range(1, G):
            to = lax.rem(g + k, G)
            copy = remote(ret.at[h, to], ret_recv.at[h, g], fs.at[h, k], fr.at[h, k], wide=to)
            copy.start()
            copies.append(copy)
        ret_recv[h, g] = ret[h, g]
        sent.extend(copies)
        return copies

    def update(c):
        rows = slice(c * LBLK, (c + 1) * LBLK)
        grad_w = jnp.dot(
            grad_ref[rows, :], xb[...].reshape(CHUNKS * span, D), preferred_element_type=jnp.float32)
        momentum = decay_rate * new_m_ref[rows, :] + grad_w
        new_m_ref[rows, :] = momentum
        new_w_ref[rows, :] = (w_ref[rows, :].astype(jnp.float32) - step_rate * momentum).astype(jnp.bfloat16)

    def take_back(h, copies):
        for copy in copies:
            copy.wait_recv()
        rows = feat // CHUNKS
        for b in range(own):
            total = jnp.zeros((rows, DBLK), jnp.float32)
            for s in range(G):
                total = total + jnp.where(asked_buf[s:s + 1, :] == b, ret_recv[h, s].astype(jnp.float32), 0.0)
            for i in range(CHUNKS):
                out_ref[i * rows:(i + 1) * rows, b * DBLK + h * half:b * DBLK + (h + 1) * half] = (
                    total[:, i * half:(i + 1) * half])

    take_slots()
    gathers = []
    for h in range(CHUNKS):
        take_wide(h)
        across, near = gather_send(h)
        if h + 1 < CHUNKS:
            passed = gather_forward(h, across)
        else:
            passed = None
        gathers.append([across, near, passed])
    loads[5].wait()

    backs = []
    pending = None
    for h in range(CHUNKS):
        across, near, passed = gathers[h]
        if passed is None:
            passed = gather_forward(h, across)
        if pending is not None:
            pending = pending + (reduce_second(pending[0], pending[1]),)
        near.wait_recv()
        for copy in passed:
            copy.wait_recv()
        compute(h)
        first = reduce_first(h)
        if pending is not None:
            backs.append(send_back(*pending))
        pending = (h, first)
    loads[6].wait()
    update(0)
    pending = pending + (reduce_second(*pending),)
    for c in range(1, lb_dev - 1):
        update(c)
    backs.append(send_back(*pending))
    for c in range(max(1, lb_dev - 1), lb_dev):
        update(c)
    for h in range(CHUNKS):
        take_back(h, backs[h])

    for copy in sent:
        copy.wait_send()


def per_device(documents, weights, momentum, positives, relocation, pair_docs, pair_labels):
    G = lax.axis_size("wide")
    N = lax.axis_size("narrow")
    labels, D = weights.shape
    lb_dev = labels // LBLK
    F = pair_docs.shape[1] // lb_dev
    docs = documents.shape[0]
    feat = D // N
    half = DBLK // CHUNKS
    part = half // N
    pos = positives.shape[1]
    outer = N // 2
    span = F * half
    table = relocation.reshape(-1, 128)
    pair_docs = pair_docs.T
    pair_labels = pair_labels.T
    positives = positives.T
    vmem = pl.BlockSpec(memory_space=pltpu.VMEM)
    hbm = pl.BlockSpec(memory_space=pltpu.HBM)
    dma = pltpu.SemaphoreType.DMA
    bf16 = jnp.bfloat16
    f32 = jnp.float32
    C = CHUNKS
    new_weights, new_momentum, out = pl.pallas_call(
        functools.partial(kernel, G, N, F),
        out_shape=(
            jax.ShapeDtypeStruct((labels, D), bf16),
            jax.ShapeDtypeStruct((labels, D), f32),
            jax.ShapeDtypeStruct((feat, docs), f32),
        ),
        in_specs=[hbm] * 7,
        out_specs=(vmem, vmem, vmem),
        scratch_shapes=[
            pltpu.VMEM(documents.shape, bf16),
            pltpu.VMEM(positives.shape, jnp.int32),
            pltpu.VMEM(table.shape, jnp.int32),
            pltpu.VMEM(pair_docs.shape, jnp.int32),
            pltpu.VMEM(pair_labels.shape, jnp.int32),
            pltpu.VMEM((labels, D), bf16),
            pltpu.VMEM((C, G, part, D), bf16),
            pltpu.VMEM((C, G, part, D), bf16),
            pltpu.VMEM((pos, docs), jnp.int32),
            pltpu.VMEM((G, pos, docs), jnp.int32),
            pltpu.VMEM((C, F, N, part, D), bf16),
            pltpu.VMEM((C, pos, span), jnp.int32),
            pltpu.VMEM((G, 128), jnp.int32),
            pltpu.VMEM((labels, C * span), bf16),
            pltpu.VMEM((C, N, feat, span), bf16),
            pltpu.VMEM((C, outer, feat, span), bf16),
            pltpu.VMEM((C, outer, feat, span), bf16),
            pltpu.VMEM((C, outer, feat, span), bf16),
            pltpu.VMEM((C, G, feat // C, DBLK), bf16),
            pltpu.VMEM((C, G, feat // C, DBLK), bf16),
            dma((7,)),
            dma((C, G)), dma((C, G)), dma((G,)), dma((G,)),
            dma((C,)), dma((C,)), dma((C, outer)), dma((C, outer)), dma((C, outer)), dma((C, outer)),
            dma((C, outer)), dma((C, outer)), dma((C, outer)), dma((C, outer)),
            dma((C, G)), dma((C, G)),
        ],
        compiler_params=pltpu.CompilerParams(
            collective_id=0, has_side_effects=True, vmem_limit_bytes=48 << 20),
    )(*(pltpu.with_memory_space_constraint(x, pltpu.HBM) for x in (
        documents, positives, table, pair_docs, pair_labels, weights, momentum)))
    return (new_weights, new_momentum, out.T)


def solution(mesh):
    in_specs = (
        P("wide", None),
        P(("wide", "narrow"), None),
        P(("wide", "narrow"), None),
        P("wide", None),
        P(),
        P(),
        P(),
    )
    out_specs = (P(("wide", "narrow"), None), P(("wide", "narrow"), None), P("wide", "narrow"))
    return jax.shard_map(
        per_device, mesh=mesh, in_specs=in_specs, out_specs=out_specs, check_vma=False
    )
```

time: 48.5 us -> 39.8 us (0.82)
  the two profiles are of different devices: /device:TPU:29 before, /device:TPU:0 now
where the time goes in v2:
time: 39.8 us; the launch traced here: 39.6 us
  Pallas kernels  35.9 us (90%)
  local copies, waits for them, and re-layouts  3.1 us (8%)
  between operations  0.64 us (2%)
    pallas_call x1, Pallas kernels, per_device(): pl.pallas_call(functools.partial(kernel, G, N, F), out_shape=(jax.ShapeDt...  35.9 us
    unnamed x3, local copies, waits for them, and re-layouts  3.1 us

profile of v2, /device:TPU:0, one launch (start us, length us, event | category | flops | bytes accessed | tf_op | source)
XLA Modules:
  0.0 39.6 jit_solution(1777656222733695409)
XLA Ops:
  0.6 35.9 %shard_map.94 = (bf16[768,768]{1,0:T(8,128)(2,1)S(1)}, f32[768,768]{1,0:T(8,128)S(1)}, f32[192,256]{1,0:T(8,128)S(1)}) custom-call(bf16[256,768]{1,0:T(8,128)(2,1)} %docs_hbm.1, s32[8,256]{1,0:T(8,128)} %bitcast.7, s32[192,128]{1,0:T(8,128)} %bitcast.6, s32[6,32]{1,0:T(8,128)} %bitcast.8, s32[6,32]{1,0:T(8,128)} %bitcast.9, bf16[768,768]{1,0:T(8,128)(2,1)} %w_hbm.1, ...), custom_call_target="tpu_custom_call" | custom-call | tf_op jit(solution)/shard_map/pallas_call | solution.py:359
  36.5 1.0 %copy.13 = bf16[768,768]{1,0:T(8,128)(2,1)} copy(bf16[768,768]{1,0:T(8,128)(2,1)S(1)} %get-tuple-element.12) | data formatting | bytes 2359296
  37.5 1.4 %copy.14 = f32[768,768]{1,0:T(8,128)} copy(f32[768,768]{1,0:T(8,128)S(1)} %get-tuple-element.13) | data formatting | bytes 4718592
  38.9 0.7 %copy.15 = f32[256,192]{0,1:T(8,128)} copy(f32[256,192]{0,1:T(8,128)S(1)} %bitcast.5) | data formatting | bytes 393216

commit v3 on v2

--- a/solution.py
+++ b/solution.py
@@ -22,6 +22,19 @@
     return pltpu.make_async_remote_copy(
         src_ref=src, dst_ref=dst, send_sem=send_sem, recv_sem=recv_sem,
         device_id=axis, device_id_type=MESH)
+
+
+def peers(g, G):
+    if G & (G - 1):
+        return [lax.rem(g + k, G) for k in range(1, G)]
+    order = []
+    for m in list(range(G // 2, G)) + list(range(1, G // 2)):
+        to = g
+        for b in range(G.bit_length() - 1):
+            if m >> b & 1:
+                to = to + (1 - 2 * ((g // (1 << b)) % 2)) * (1 << b)
+        order.append(to)
+    return order
 
 
 def kernel(G, N, F, docs_hbm, pos_hbm, table_hbm, pd_hbm, pl_hbm, w_hbm, m_hbm,
@@ -45,25 +58,24 @@
     partner = n + 1 - 2 * (n % 2)
     sent = []
 
+    order = list(enumerate(peers(g, G), 1))
     barrier = pltpu.get_barrier_semaphore()
-    for k in range(1, G):
-        pl.semaphore_signal(barrier, inc=1, device_id={"wide": lax.rem(g + k, G)}, device_id_type=MESH)
+    for k, to in order:
+        pl.semaphore_signal(barrier, inc=1, device_id={"wide": to}, device_id_type=MESH)
     for k in range(1, N):
         pl.semaphore_signal(barrier, inc=1, device_id={"narrow": lax.rem(n + k, N)}, device_id_type=MESH)
 
     loads = [
         pltpu.make_async_copy(src, dst, in_sem.at[i])
         for i, (src, dst) in enumerate((
-            (pd_hbm, pd_ref), (pl_hbm, pl_ref), (docs_hbm, docs_ref), (pos_hbm, pos_ref),
+            (pd_hbm, pd_ref), (docs_hbm, docs_ref), (pl_hbm, pl_ref), (pos_hbm, pos_ref),
             (table_hbm, table_ref), (w_hbm, w_ref), (m_hbm, new_m_ref)))
     ]
     for load in loads:
         load.start()
     loads[0].wait()
-    loads[1].wait()
 
     pair_docs = pd_ref[...]
-    pair_labels = pl_ref[...]
     device_of = lax.broadcasted_iota(jnp.int32, pair_docs.shape, 1)
     group_of = device_of // N
     local = jnp.where((pair_docs >= 0) & (pair_docs // own == g), pair_docs % own, -1)
@@ -84,7 +96,7 @@
         blocks.append(last)
     owner = [b // own for b in blocks]
 
-    loads[2].wait()
+    loads[1].wait()
     for h in range(CHUNKS):
         rows = [
             docs_ref[pl.ds(pl.multiple_of(b * DBLK + h * half + n * part, part), part), :]
@@ -97,6 +109,17 @@
     for d in range(G):
         asked_buf[d:d + 1, :] = jnp.broadcast_to(asked[d], (1, asked_buf.shape[1]))
 
+    pl.semaphore_wait(barrier, G - 1 + N - 1)
+
+    wide_copies = []
+    for h in range(CHUNKS):
+        copies = []
+        for k, to in order:
+            copy = remote(send_buf.at[h, to], recv_buf.at[h, g], ws.at[h, k], wr.at[h, k], wide=to)
+            copy.start()
+            copies.append(copy)
+        wide_copies.append(copies)
+        sent.extend(copies)
     loads[3].wait()
     loads[4].wait()
     table = table_ref[...]
@@ -119,24 +142,11 @@
             total = total + jnp.sum(jnp.where(low, rows, 0.0), axis=0, keepdims=True) * float(1 << (8 * i))
         slot_buf[p:p + 1, :] = total.astype(jnp.int32)
 
-    pl.semaphore_wait(barrier, G - 1 + N - 1)
-
     slot_copies = []
-    for k in range(1, G):
-        to = lax.rem(g + k, G)
+    for k, to in order:
         copy = remote(slot_buf, slot_recv.at[g], ss.at[k], sr.at[k], wide=to)
         copy.start()
         slot_copies.append(copy)
-    wide_copies = []
-    for h in range(CHUNKS):
-        copies = []
-        for k in range(1, G):
-            to = lax.rem(g + k, G)
-            copy = remote(send_buf.at[h, to], recv_buf.at[h, g], ws.at[h, k], wr.at[h, k], wide=to)
-            copy.start()
-            copies.append(copy)
-        wide_copies.append(copies)
-        sent.extend(copies)
     sent.extend(slot_copies)
     slot_recv[g] = slot_buf[...]
     for h in range(CHUNKS):
@@ -187,6 +197,8 @@
         sent.extend(passed)
         return passed
 
+    loads[2].wait()
+    pair_labels = pl_ref[...]
     me = g * N + n
     label_base = me * labels
     step = 4 if F % 4 == 0 else 2 if F % 2 == 0 else 1
@@ -261,8 +273,7 @@
                 back = jnp.where(owner[j] == d, packed[j], back)
             ret[h, d] = back
         copies = []
-        for k in range(1, G):
-            to = lax.rem(g + k, G)
+        for k, to in order:
             copy = remote(ret.at[h, to], ret_recv.at[h, g], fs.at[h, k], fr.at[h, k], wide=to)
             copy.start()
             copies.append(copy)
@@ -290,7 +301,6 @@
                 out_ref[i * rows:(i + 1) * rows, b * DBLK + h * half:b * DBLK + (h + 1) * half] = (
                     total[:, i * half:(i + 1) * half])
 
-    take_slots()
     gathers = []
     for h in range(CHUNKS):
         take_wide(h)
@@ -301,6 +311,7 @@
             passed = None
         gathers.append([across, near, passed])
     loads[5].wait()
+    take_slots()
 
     backs = []
     pending = None
@@ -331,6 +342,16 @@
 
     for copy in sent:
         copy.wait_send()
+
+
+def store_kernel(a_ref, b_ref, c_ref, a_out, b_out, c_out, sem):
+    stores = [
+        pltpu.make_async_copy(src, dst, sem.at[i])
+        for i, (src, dst) in enumerate(((b_ref, b_out), (a_ref, a_out), (c_ref, c_out)))]
+    for store in stores:
+        store.start()
+    for store in stores:
+        store.wait()
 
 
 def per_device(documents, weights, momentum, positives, relocation, pair_docs, pair_labels):
@@ -396,6 +417,15 @@
             collective_id=0, has_side_effects=True, vmem_limit_bytes=48 << 20),
     )(*(pltpu.with_memory_space_constraint(x, pltpu.HBM) for x in (
         documents, positives, table, pair_docs, pair_labels, weights, momentum)))
+    results = (new_weights, new_momentum, out)
+    new_weights, new_momentum, out = pl.pallas_call(
+        store_kernel,
+        out_shape=[jax.ShapeDtypeStruct(x.shape, x.dtype) for x in results],
+        in_specs=[vmem] * 3,
+        out_specs=[hbm] * 3,
+        scratch_shapes=[dma((3,))],
+        compiler_params=pltpu.CompilerParams(vmem_limit_bytes=8 << 20),
+    )(*results)
     return (new_weights, new_momentum, out.T)
 
 

time: 39.8 us -> 38.5 us (0.967)
  local copies, waits for them, and re-layouts: 3.1 us -> 0 us
  Pallas kernels: 35.9 us -> 37.7 us
    unnamed x3 -> x0, local copies, waits for them, and re-layouts: 3.1 us -> none
    pallas_call x0 -> x1, Pallas kernels: none -> 1.87 us  [per_device(): pl.pallas_call(store_kernel, out_shape=[jax.ShapeDtypeStruct(x.shape, x.d...]
where the time goes in v3:
time: 38.5 us; the launch traced here: 38.4 us
  Pallas kernels  37.7 us (98%)
  between operations  0.64 us (2%)
    pallas_call x1, Pallas kernels, per_device(): pl.pallas_call(functools.partial(kernel, G, N, F), out_shape=(jax.ShapeDt...  35.8 us
    pallas_call x1, Pallas kernels, per_device(): pl.pallas_call(store_kernel, out_shape=[jax.ShapeDtypeStruct(x.shape, x.d...  1.87 us

profile of v3, /device:TPU:0, one launch (start us, length us, event | category | flops | bytes accessed | tf_op | source)
XLA Modules:
  0.0 38.4 jit_solution(15987590865155050654)
XLA Ops:
  0.6 35.8 %shard_map.94 = (bf16[768,768]{1,0:T(8,128)(2,1)S(1)}, f32[768,768]{1,0:T(8,128)S(1)}, f32[192,256]{1,0:T(8,128)S(1)}) custom-call(bf16[256,768]{1,0:T(8,128)(2,1)} %docs_hbm.1, s32[8,256]{1,0:T(8,128)} %bitcast.6, s32[192,128]{1,0:T(8,128)} %bitcast.5, s32[6,32]{1,0:T(8,128)} %bitcast.7, s32[6,32]{1,0:T(8,128)} %bitcast.8, bf16[768,768]{1,0:T(8,128)(2,1)} %w_hbm.1, ...), custom_call_target="tpu_custom_call" | custom-call | tf_op jit(solution)/shard_map/pallas_call | solution.py:380
  36.5 1.9 %shard_map.95 = (bf16[768,768]{1,0:T(8,128)(2,1)}, f32[768,768]{1,0:T(8,128)}, f32[192,256]{1,0:T(8,128)}) custom-call(bf16[768,768]{1,0:T(8,128)(2,1)S(1)} %get-tuple-element.9.a_ref, f32[768,768]{1,0:T(8,128)S(1)} %get-tuple-element.10.b_ref, f32[192,256]{1,0:T(8,128)S(1)} %get-tuple-element.11.c_ref), custom_call_target="tpu_custom_call" | custom-call | tf_op jit(solution)/shard_map/pallas_call | solution.py:421
